TPU v7x, 256 devices: a whole 4x4x8 slice. The times are simulated.
256 devices in a mesh: grp: 4 (over z_hi, core), dev: 64 (over x, y, z_lo).
Axes of the slice: x: 4, y: 4, z: 8 (z_hi: 2, z_lo: 4; z = z_hi * 4 + z_lo), core: 2. Of those that a mesh axis runs over, the one named last changes fastest.
Arguments:
- wavefield: float32 [256, 2, 128, 2048], P(('grp', 'dev')), may hold values from -6 to 6
- measured: float32 [256, 128, 2048], P(('grp', 'dev')), may hold values from 0.5 to 4
- leaf_map: float32 [256, 2, 128, 128], P(('grp', 'dev')), may hold values from -0.375 to 0.375
- factors: float32 [8, 256, 2, 128, 128], P(None, ('grp', 'dev')), may hold values from -0.375 to 0.375
- closing: float32 [256, 2, 128, 128], P(('grp', 'dev')), may hold values from -0.375 to 0.375
- box_perm: int32 [256, 2048], P(('grp', 'dev')), may hold values from 0 to 2047, each once within a row
- factor_order: int32 [8], replicated, may hold values from 0 to 7, each once
Outputs:
- projected: float32 [256, 2, 128, 2048], P(('grp', 'dev'))
Inputs may be any that keep to these rules, and one draw needn't show every extreme that they name: `box_perm`: each row is a permutation of 0 .. 2047. `factor_order`: a permutation of 0 .. 7.
All inputs are finite; a program needn't handle non-finite values.
Results may differ from a plain program's by a relative error of at most 0.00018.
Values sent between devices are 32-bit elements; how exact they have to be, the bound alone decides.
A program may use at most 64 MiB of HBM per device.

v0:
```python
import functools

import jax
import jax.numpy as jnp
from jax import lax
from jax.experimental import pallas as pl
from jax.experimental.pallas import tpu as pltpu
from jax.sharding import PartitionSpec as P

MESH = pl.DeviceIdType.MESH
LEVELS = 8
SWITCH = LEVELS // 2
WIDTH = 256
AHEAD = 2
LAG_A = 1
LAG_B = 1


def kernel(
    dev_bits, order_ref, perm_ref, field_hbm, measured_hbm, leaf_hbm, factors_hbm, closing_hbm, out_hbm,
    field, measured, leaf, factors, closing, weights, onehot, outgoing, held, parts, result,
    in_sem, chunk_sem, send_sem, recv_sem, out_sem, turn_sem,
):
    chunks, half, width = outgoing.shape[1:]
    slots = half // 2
    full = 2 * half
    f32, bf16 = jnp.float32, jnp.bfloat16
    grp, dev = lax.axis_index("grp"), lax.axis_index("dev")

    def bit_of(level):
        if level < 2:
            return (grp // (2 >> level)) % 2
        return (dev // (1 << (level - 2) % dev_bits)) % 2

    bits = [bit_of(level) for level in range(LEVELS)]

    def partner(level):
        turn = 1 - 2 * bits[level]
        if level < 2:
            return (grp + turn * (2 >> level), dev)
        return (grp, dev + turn * (1 << (level - 2) % dev_bits))

    def columns(chunk):
        return pl.ds(pl.multiple_of(chunk * width, width), width)

    def remote(level, chunk):
        return pltpu.make_async_remote_copy(
            src_ref=outgoing.at[level, chunk],
            dst_ref=held.at[level, chunk, pl.ds(half, half)],
            send_sem=send_sem.at[level, chunk],
            recv_sem=recv_sem.at[level, chunk],
            device_id=partner(level),
            device_id_type=MESH,
        )

    def fetch_field(chunk):
        return pltpu.make_async_copy(
            field_hbm.at[0, :, :, columns(chunk)], field.at[:, :, columns(chunk)], chunk_sem.at[chunk]
        )

    def put_result(chunk):
        return pltpu.make_async_copy(
            result.at[chunk], out_hbm.at[0, :, :, columns(chunk)], out_sem.at[chunk]
        )

    barrier = pltpu.get_barrier_semaphore()
    for level in range(LEVELS):
        pl.semaphore_signal(barrier, inc=1, device_id=partner(level), device_id_type=MESH)

    fetch_leaf = pltpu.make_async_copy(leaf_hbm.at[0], leaf, in_sem.at[0])
    fetch_leaf.start()
    for chunk in range(chunks):
        fetch_field(chunk).start()
    fetch_factors = pltpu.make_async_copy(factors_hbm.at[:, 0], factors, in_sem.at[1])
    fetch_factors.start()
    fetch_closing = pltpu.make_async_copy(closing_hbm.at[0], closing, in_sem.at[2])
    fetch_closing.start()
    fetch_measured = pltpu.make_async_copy(measured_hbm.at[0], measured, in_sem.at[3])
    fetch_measured.start()

    def store_weights(which, row, left, right):
        rows = left.shape[0]
        for side, block in ((0, left), (half, right)):
            high = block.astype(bf16)
            low = (block - high.astype(f32)).astype(bf16)
            weights[which, row : row + rows, side : side + half] = high
            weights[which, full + row : full + row + rows, side : side + half] = low

    def prepare(which, load, in_bit, out_bit):
        if out_bit is None:
            blocks = [(0, half, 0, half)]
        else:
            blocks = [
                (0, slots, (1 - out_bit) * slots, slots),
                (half, half + slots, out_bit * slots, slots),
            ]
        for real_row, imag_row, start, rows in blocks:
            if not isinstance(start, int):
                start = pl.multiple_of(start, slots)
            real = load(0, pl.ds(start, rows))
            imag = load(1, pl.ds(start, rows))
            if in_bit is None:
                store_weights(which, real_row, real, -imag)
                store_weights(which, imag_row, imag, real)
            else:
                first = lax.broadcasted_iota(jnp.int32, real.shape, 1) < slots
                real_over, imag_over = pltpu.roll(real, slots, 1), pltpu.roll(imag, slots, 1)
                own_first = in_bit == 0
                real, real_over = jnp.where(own_first, real, real_over), jnp.where(own_first, real_over, real)
                imag, imag_over = jnp.where(own_first, imag, imag_over), jnp.where(own_first, imag_over, imag)
                store_weights(
                    which, real_row, jnp.where(first, real, -imag_over), jnp.where(first, real_over, -imag)
                )
                store_weights(
                    which, imag_row, jnp.where(first, imag, real_over), jnp.where(first, imag_over, real)
                )

    def product(which, vectors):
        high = vectors.astype(bf16)
        low = (vectors - high.astype(f32)).astype(bf16)
        both = jnp.dot(weights[which], high, preferred_element_type=f32)
        rest = jnp.dot(weights[which, :full], low, preferred_element_type=f32)
        return both[:full] + (both[full:] + rest)

    def hand_on(level, chunk, coeffs):
        outgoing[level, chunk] = coeffs[:half]
        held[level, chunk, :half] = coeffs[half:]

    fetch_leaf.wait()
    prepare(0, lambda part, rows: leaf[part, rows, :], None, bits[0])
    pl.semaphore_wait(barrier, LEVELS)

    def open_chunk(chunk, carry):
        fetch_field(chunk).wait()
        vectors = field[:, :, columns(chunk)].reshape(full, width)
        hand_on(0, chunk, product(0, vectors))
        remote(0, chunk).start()
        return carry

    lax.fori_loop(0, chunks, open_chunk, 0)

    fetch_factors.wait()
    fetch_closing.wait()
    for level in range(LEVELS):
        pick = order_ref[level]
        prepare(
            1 + level,
            lambda part, rows, pick=pick: factors[pick, part, rows, :],
            bits[level],
            bits[level + 1] if level + 1 < LEVELS else None,
        )
    prepare(1 + LEVELS, lambda part, rows: closing[part, rows, :], None, None)

    def fill_onehot(step, carry):
        chunk, block = step // chunks, step % chunks
        wanted = perm_ref[:, columns(chunk)]
        source = lax.broadcasted_iota(jnp.int32, (width, width), 0) + block * width
        onehot[chunk, columns(block), :] = jnp.where(source == wanted, 1.0, 0.0).astype(bf16)
        return carry

    lax.fori_loop(0, chunks * chunks, fill_onehot, 0)
    fetch_measured.wait()

    def arrive(level, chunk):
        remote(level, chunk).wait_recv()
        return product(1 + level, held[level, chunk])

    def when_in_range(chunk, body):
        pl.when(jnp.logical_and(chunk >= 0, chunk < chunks))(lambda: body(chunk))

    def level_0(chunk):
        hand_on(1, chunk, arrive(0, chunk))
        remote(1, chunk).start()

    def level_1(chunk):
        hand_on(2, chunk, arrive(1, chunk))

    def level_2(chunk):
        hand_on(3, chunk, arrive(2, chunk))
        remote(3, chunk).start()

    def level_3(chunk):
        coeffs = arrive(3, chunk)
        high = coeffs.astype(bf16)
        parts[:full, columns(chunk)] = high
        parts[full:, columns(chunk)] = (coeffs - high.astype(f32)).astype(bf16)

    def switch(chunk):
        both = jnp.dot(parts[...], onehot[chunk], preferred_element_type=f32)
        hand_on(4, chunk, both[:full] + both[full:])
        remote(4, chunk).start()

    def middle(level, chunk):
        hand_on(level + 1, chunk, arrive(level, chunk))
        remote(level + 1, chunk).start()

    def level_7(chunk):
        image = product(1 + LEVELS, arrive(7, chunk))
        real, imag = image[:half], image[half:]
        scale = measured[:, columns(chunk)] * lax.rsqrt(jnp.maximum(real * real + imag * imag, 0.25))
        result[chunk, 0] = real * scale
        result[chunk, 1] = imag * scale
        put_result(chunk).start()

    def near(step, carry):
        when_in_range(step, level_0)
        when_in_range(step - 1, level_1)
        return carry

    lax.fori_loop(0, chunks + 1, near, 0)

    first_core = grp % 2 == 0

    @pl.when(jnp.logical_not(first_core))
    def _():
        pl.semaphore_wait(turn_sem, 1)

    for chunk in range(AHEAD):
        remote(2, chunk).start()

    def along(step, carry):
        def send_more(chunk):
            remote(2, chunk).start()

        when_in_range(step, level_2)

        @pl.when(jnp.logical_and(first_core, step == chunks - 1))
        def _():
            pl.semaphore_signal(turn_sem, inc=1, device_id=partner(1), device_id_type=MESH)

        pl.when(step + AHEAD < chunks)(lambda: send_more(step + AHEAD))
        when_in_range(step - LAG_A, level_3)
        return carry

    lax.fori_loop(0, chunks + LAG_A, along, 0)

    def across(step, carry):
        when_in_range(step, switch)
        when_in_range(step - LAG_B, functools.partial(middle, 4))
        when_in_range(step - 2 * LAG_B, functools.partial(middle, 5))
        when_in_range(step - 3 * LAG_B, functools.partial(middle, 6))
        when_in_range(step - 4 * LAG_B, level_7)
        return carry

    lax.fori_loop(0, chunks + 4 * LAG_B, across, 0)

    def finish(chunk, carry):
        put_result(chunk).wait()
        for level in range(LEVELS):
            remote(level, chunk).wait_send()
        return carry

    lax.fori_loop(0, chunks, finish, 0)


def solution(mesh):
    dev_bits = mesh.shape["dev"].bit_length() - 1

    def per_device(wavefield, measured, leaf_map, factors, closing, box_perm, factor_order):
        _, _, half, boxes = wavefield.shape
        width = min(WIDTH, boxes)
        chunks = boxes // width
        full = 2 * half
        f32, bf16 = jnp.float32, jnp.bfloat16
        anywhere = pl.BlockSpec(memory_space=pl.ANY)
        return pl.pallas_call(
            functools.partial(kernel, dev_bits),
            out_shape=jax.ShapeDtypeStruct(wavefield.shape, f32),
            in_specs=[
                pl.BlockSpec(memory_space=pltpu.SMEM),
                pl.BlockSpec(memory_space=pltpu.VMEM),
            ]
            + [anywhere] * 5,
            out_specs=anywhere,
            scratch_shapes=[
                pltpu.VMEM((2, half, boxes), f32),
                pltpu.VMEM((half, boxes), f32),
                pltpu.VMEM((2, half, half), f32),
                pltpu.VMEM((LEVELS, 2, half, half), f32),
                pltpu.VMEM((2, half, half), f32),
                pltpu.VMEM((LEVELS + 2, 2 * full, full), bf16),
                pltpu.VMEM((chunks, boxes, width), bf16),
                pltpu.VMEM((LEVELS, chunks, half, width), f32),
                pltpu.VMEM((LEVELS, chunks, full, width), f32),
                pltpu.VMEM((2 * full, boxes), bf16),
                pltpu.VMEM((chunks, 2, half, width), f32),
                pltpu.SemaphoreType.DMA((4,)),
                pltpu.SemaphoreType.DMA((chunks,)),
                pltpu.SemaphoreType.DMA((LEVELS, chunks)),
                pltpu.SemaphoreType.DMA((LEVELS, chunks)),
                pltpu.SemaphoreType.DMA((chunks,)),
                pltpu.SemaphoreType.REGULAR,
            ],
            compiler_params=pltpu.CompilerParams(
                collective_id=0, has_side_effects=True, vmem_limit_bytes=60 * 2**20
            ),
        )(factor_order, box_perm, wavefield, measured, leaf_map, factors, closing)

    return jax.shard_map(
        per_device,
        mesh=mesh,
        in_specs=(
            P(("grp", "dev"), None, None, None),
            P(("grp", "dev"), None, None),
            P(("grp", "dev"), None, None, None),
            P(None, ("grp", "dev"), None, None, None),
            P(("grp", "dev"), None, None, None),
            P(("grp", "dev"), None),
            P(),
        ),
        out_specs=P(("grp", "dev"), None, None, None),
        check_vma=False,
    )
```

profile of v0, /device:TPU:1, one launch (start us, length us, event | category | flops | bytes accessed | tf_op | source)
XLA Modules:
  0.0 174.2 jit_solution(8401964333514024474)
XLA Ops:
  0.0 171.1 %shard_map.73 = f32[1,2,128,2048]{3,2,1,0:T(8,128)} custom-call(s32[8]{0:T(128)} %order_ref.1, s32[1,2048]{1,0:T(1,128)} %perm_ref.1, f32[1,2,128,2048]{3,2,1,0:T(8,128)} %field_hbm.1, f32[1,128,2048]{2,1,0:T(8,128)} %measured_hbm.1, f32[1,2,128,128]{3,2,1,0:T(8,128)} %leaf_hbm.1, f32[8,1,2,128,128]{4,3,2,1,0:T(8,128)} %factors_hbm.1, ...), custom_call_target="tpu_custom_call" | custom-call | tf_op jit(solution)/shard_map/pallas_call | solution.py:266
  171.1 3.1 %copy.9 = f32[1,2,128,2048]{3,2,1,0:T(8,128)} copy(f32[1,2,128,2048]{3,2,1,0:T(8,128)} %shard_map.73) | data formatting | bytes 4194304
where the time goes:
time: 174 us
  Pallas kernels  171 us (98%)
  local copies, waits for them, and re-layouts  3.14 us (2%)
    pallas_call x1, Pallas kernels, per_device(): pl.pallas_call(functools.partial(kernel, dev_bits), out_shape=jax.ShapeDt...  171 us

commit v1 on v0

v1 whole, which is shorter than its diff:
```python
import functools

import jax
import jax.numpy as jnp
from jax import lax
from jax.experimental import pallas as pl
from jax.experimental.pallas import tpu as pltpu
from jax.sharding import PartitionSpec as P

MESH = pl.DeviceIdType.MESH
LEVELS = 8
VMEM_BYTES = 67043328
SWITCH = LEVELS // 2
WIDTH = 256
WIDTH_B = 128
EARLY = 4
AHEAD = 3
SPARE = 1
BEFORE = 0
LAG_2 = 3
LAG_3 = 2
LAG_4 = 3
LAG_5 = 3
LAG_6 = 3
LAG_7 = 3


def kernel(
    dev_bits, order_ref, perm_ref, field_hbm, leaf_hbm, factors_hbm, closing_hbm, image_hbm,
    field, leaf, factors, closing, weights, onehot, near_out, near_held, far_out, far_held, parts, image,
    in_sem, chunk_sem, near_send, near_recv, far_send, far_recv, out_sem, turn_sem,
):
    chunks, half, width = near_out.shape[1:]
    chunks_b, _, width_b = far_out.shape[1:]
    slots = half // 2
    full = 2 * half
    f32, bf16 = jnp.float32, jnp.bfloat16
    grp, dev = lax.axis_index("grp"), lax.axis_index("dev")

    def bit_of(level):
        if level < 2:
            return (grp // (2 >> level)) % 2
        return (dev // (1 << (level - 2) % dev_bits)) % 2

    bits = [bit_of(level) for level in range(LEVELS)]

    def partner(level):
        turn = 1 - 2 * bits[level]
        if level < 2:
            return (grp + turn * (2 >> level), dev)
        return (grp, dev + turn * (1 << (level - 2) % dev_bits))

    def columns(chunk, width=width):
        return pl.ds(pl.multiple_of(chunk * width, width), width)

    def stage(level):
        if level < SWITCH:
            return near_out.at[level], near_held.at[level], near_send.at[level], near_recv.at[level]
        level -= SWITCH
        return far_out.at[level], far_held.at[level], far_send.at[level], far_recv.at[level]

    def remote(level, chunk):
        outgoing, held, send_sem, recv_sem = stage(level)
        return pltpu.make_async_remote_copy(
            src_ref=outgoing.at[chunk],
            dst_ref=held.at[chunk, pl.ds(half, half)],
            send_sem=send_sem.at[chunk],
            recv_sem=recv_sem.at[chunk],
            device_id=partner(level),
            device_id_type=MESH,
        )

    def fetch_field(chunk):
        return pltpu.make_async_copy(
            field_hbm.at[0, :, :, columns(chunk)], field.at[:, :, columns(chunk)], chunk_sem.at[chunk]
        )

    def put_image(chunk):
        return pltpu.make_async_copy(
            image.at[chunk], image_hbm.at[0, :, :, columns(chunk, width_b)], out_sem.at[chunk]
        )

    barrier = pltpu.get_barrier_semaphore()
    for level in range(LEVELS):
        pl.semaphore_signal(barrier, inc=1, device_id=partner(level), device_id_type=MESH)

    fetch_leaf = pltpu.make_async_copy(leaf_hbm.at[0], leaf, in_sem.at[0])
    fetch_leaf.start()
    for chunk in range(chunks):
        fetch_field(chunk).start()
    fetch_factors = pltpu.make_async_copy(factors_hbm.at[:, 0], factors, in_sem.at[1])
    fetch_factors.start()
    fetch_closing = pltpu.make_async_copy(closing_hbm.at[0], closing, in_sem.at[2])
    fetch_closing.start()

    def store_weights(which, row, left, right):
        rows = left.shape[0]
        for side, block in ((0, left), (half, right)):
            high = block.astype(bf16)
            low = (block - high.astype(f32)).astype(bf16)
            weights[which, row : row + rows, side : side + half] = high
            weights[which, full + row : full + row + rows, side : side + half] = low

    def prepare(which, load, in_bit, out_bit):
        if out_bit is None:
            blocks = [(0, half, 0, half)]
        else:
            blocks = [
                (0, slots, (1 - out_bit) * slots, slots),
                (half, half + slots, out_bit * slots, slots),
            ]
        for real_row, imag_row, start, rows in blocks:
            if not isinstance(start, int):
                start = pl.multiple_of(start, slots)
            real = load(0, pl.ds(start, rows))
            imag = load(1, pl.ds(start, rows))
            if in_bit is None:
                store_weights(which, real_row, real, -imag)
                store_weights(which, imag_row, imag, real)
            else:
                first = lax.broadcasted_iota(jnp.int32, real.shape, 1) < slots
                real_over, imag_over = pltpu.roll(real, slots, 1), pltpu.roll(imag, slots, 1)
                own_first = in_bit == 0
                real, real_over = jnp.where(own_first, real, real_over), jnp.where(own_first, real_over, real)
                imag, imag_over = jnp.where(own_first, imag, imag_over), jnp.where(own_first, imag_over, imag)
                store_weights(
                    which, real_row, jnp.where(first, real, -imag_over), jnp.where(first, real_over, -imag)
                )
                store_weights(
                    which, imag_row, jnp.where(first, imag, real_over), jnp.where(first, imag_over, real)
                )

    def product(which, vectors):
        high = vectors.astype(bf16)
        low = (vectors - high.astype(f32)).astype(bf16)
        both = jnp.dot(weights[which], high, preferred_element_type=f32)
        rest = jnp.dot(weights[which, :full], low, preferred_element_type=f32)
        return both[:full] + (both[full:] + rest)

    def hand_on(level, chunk, coeffs):
        outgoing, held, _, _ = stage(level)
        outgoing[chunk] = coeffs[:half]
        held[chunk, :half] = coeffs[half:]

    fetch_leaf.wait()
    prepare(0, lambda part, rows: leaf[part, rows, :], None, bits[0])
    pl.semaphore_wait(barrier, LEVELS)

    def open_chunk(chunk, carry):
        fetch_field(chunk).wait()
        vectors = field[:, :, columns(chunk)].reshape(full, width)
        hand_on(0, chunk, product(0, vectors))
        pl.when(chunk < EARLY)(lambda: remote(0, chunk).start())
        return carry

    lax.fori_loop(0, chunks, open_chunk, 0)

    fetch_factors.wait()
    fetch_closing.wait()
    for level in range(LEVELS):
        pick = order_ref[level]
        prepare(
            1 + level,
            lambda part, rows, pick=pick: factors[pick, part, rows, :],
            bits[level],
            bits[level + 1] if level + 1 < LEVELS else None,
        )
    prepare(0, lambda part, rows: closing[part, rows, :], None, None)
    last = weights[LEVELS, :full].astype(f32) + weights[LEVELS, full:].astype(f32)
    last = product(0, last)
    high = last.astype(bf16)
    weights[LEVELS, :full] = high
    weights[LEVELS, full:] = (last - high.astype(f32)).astype(bf16)

    def fill_onehot(step, carry):
        chunk, block = step // chunks, step % chunks
        wanted = perm_ref[:, columns(chunk)]
        source = lax.broadcasted_iota(jnp.int32, (width, width), 0) + block * width
        onehot[chunk, columns(block), :] = jnp.where(source == wanted, 1.0, 0.0).astype(bf16)
        return carry

    lax.fori_loop(0, chunks * chunks, fill_onehot, 0)

    def clear(chunk, carry):
        hand_on(SWITCH, chunk, jnp.zeros((full, width_b), f32))
        return carry

    lax.fori_loop(0, chunks_b, clear, 0)

    def arrive(level, chunk):
        remote(level, chunk).wait_recv()
        return product(1 + level, stage(level)[1][chunk])

    def when_in_range(chunk, body, chunks=chunks):
        pl.when(jnp.logical_and(chunk >= 0, chunk < chunks))(lambda: body(chunk))

    def level_0(chunk):
        hand_on(1, chunk, arrive(0, chunk))
        remote(1, chunk).start()

    def level_1(chunk):
        hand_on(2, chunk, arrive(1, chunk))

    def level_2(chunk):
        hand_on(3, chunk, arrive(2, chunk))
        remote(3, chunk).start()

    def level_3(chunk):
        coeffs = arrive(3, chunk)
        high = coeffs.astype(bf16)
        parts[:full] = high
        parts[full:] = (coeffs - high.astype(f32)).astype(bf16)

        def place(target, carry):
            both = jnp.dot(parts[...], onehot[target, columns(chunk), :], preferred_element_type=f32)
            both = both[:full] + both[full:]
            for piece in range(width // width_b):
                which = target * (width // width_b) + piece
                block = both[:, piece * width_b : (piece + 1) * width_b]
                far_out[0, which] += block[:half]
                far_held[0, which, :half] += block[half:]
            return carry

        lax.fori_loop(0, chunks, place, 0, unroll=2)

    def switch(chunk):
        remote(SWITCH, chunk).start()

    def middle(level, chunk):
        hand_on(level + 1, chunk, arrive(level, chunk))
        remote(level + 1, chunk).start()

    def level_7(chunk):
        coeffs = arrive(7, chunk)
        image[chunk, 0] = coeffs[:half]
        image[chunk, 1] = coeffs[half:]
        put_image(chunk).start()

    first_core = grp % 2 == 0

    def send(level, chunk):
        remote(level, chunk).start()

    def near(step, carry):
        when_in_range(step, level_0)
        pl.when(step + EARLY < chunks)(lambda: send(0, step + EARLY))
        when_in_range(step - 1, level_1)
        return carry

    def along(step, carry):
        when_in_range(step, level_2)

        @pl.when(jnp.logical_and(first_core, step == chunks - SPARE))
        def _():
            pl.semaphore_signal(turn_sem, inc=1, device_id=partner(1), device_id_type=MESH)

        when_in_range(step - LAG_3, level_3)
        return carry

    @pl.when(first_core)
    def _():
        def both(step, carry):
            near(step, carry)
            when_in_range(step - 1, functools.partial(send, 2))
            return along(step - LAG_2, carry)

        lax.fori_loop(0, chunks + LAG_2 + LAG_3, both, 0)

    @pl.when(jnp.logical_not(first_core))
    def _():
        def open_turn():
            for chunk in range(AHEAD):
                send(2, chunk)

        lax.fori_loop(0, chunks + 1, near, 0)
        if BEFORE:
            open_turn()
        pl.semaphore_wait(turn_sem, 1)
        if not BEFORE:
            open_turn()

        def rest(step, carry):
            along(step, carry)
            pl.when(step + AHEAD < chunks)(lambda: send(2, step + AHEAD))
            return carry

        lax.fori_loop(0, chunks + LAG_3, rest, 0)

    def leave(levels, chunk):
        for level in levels:
            remote(level, chunk).wait_send()

    lags = (0, LAG_4, LAG_4 + LAG_5, LAG_4 + LAG_5 + LAG_6, LAG_4 + LAG_5 + LAG_6 + LAG_7)

    def across(step, carry):
        when_in_range(step, switch, chunks_b)
        when_in_range(step - lags[1], functools.partial(middle, 4), chunks_b)
        when_in_range(step - lags[2], functools.partial(middle, 5), chunks_b)
        when_in_range(step - lags[3], functools.partial(middle, 6), chunks_b)
        when_in_range(step - lags[4], level_7, chunks_b)
        when_in_range(step, functools.partial(leave, range(SWITCH)))
        when_in_range(step - lags[4], functools.partial(leave, range(SWITCH, LEVELS)), chunks_b)
        return carry

    lax.fori_loop(0, chunks_b + lags[4], across, 0)

    def finish(chunk, carry):
        put_image(chunk).wait()
        return carry

    lax.fori_loop(0, chunks_b, finish, 0)


def project(image_hbm, measured_hbm, out_hbm, image, measured, in_sem, measured_sem, out_sem):
    chunks, _, _, width = image.shape

    def columns(chunk):
        return pl.ds(pl.multiple_of(chunk * width, width), width)

    def get(chunk):
        return pltpu.make_async_copy(image_hbm.at[0, :, :, columns(chunk)], image.at[chunk], in_sem.at[chunk])

    def put(chunk):
        return pltpu.make_async_copy(image.at[chunk], out_hbm.at[0, :, :, columns(chunk)], out_sem.at[chunk])

    def get_measured(chunk):
        return pltpu.make_async_copy(
            measured_hbm.at[0, :, columns(chunk)], measured.at[chunk], measured_sem.at[chunk]
        )

    for chunk in range(chunks):
        get(chunk).start()
        get_measured(chunk).start()

    def step(chunk, carry):
        get(chunk).wait()
        get_measured(chunk).wait()
        real, imag = image[chunk, 0], image[chunk, 1]
        scale = measured[chunk] * lax.rsqrt(jnp.maximum(real * real + imag * imag, 0.25))
        image[chunk, 0] = real * scale
        image[chunk, 1] = imag * scale
        put(chunk).start()
        return carry

    def finish(chunk, carry):
        put(chunk).wait()
        return carry

    lax.fori_loop(0, chunks, step, 0)
    lax.fori_loop(0, chunks, finish, 0)


def solution(mesh):
    dev_bits = mesh.shape["dev"].bit_length() - 1

    def per_device(wavefield, measured, leaf_map, factors, closing, box_perm, factor_order):
        _, _, half, boxes = wavefield.shape
        width, width_b = min(WIDTH, boxes), min(WIDTH_B, boxes)
        chunks, chunks_b = boxes // width, boxes // width_b
        full = 2 * half
        f32, bf16 = jnp.float32, jnp.bfloat16
        in_hbm = pl.BlockSpec(memory_space=pltpu.HBM)
        in_vmem = pl.BlockSpec(memory_space=pltpu.VMEM)
        image = pl.pallas_call(
            functools.partial(kernel, dev_bits),
            out_shape=jax.ShapeDtypeStruct(wavefield.shape, f32),
            in_specs=[
                pl.BlockSpec(memory_space=pltpu.SMEM),
                in_vmem,
            ]
            + [in_hbm] * 4,
            out_specs=in_hbm,
            scratch_shapes=[
                pltpu.VMEM((2, half, boxes), f32),
                pltpu.VMEM((2, half, half), f32),
                pltpu.VMEM((LEVELS, 2, half, half), f32),
                pltpu.VMEM((2, half, half), f32),
                pltpu.VMEM((LEVELS + 1, 2 * full, full), bf16),
                pltpu.VMEM((chunks, boxes, width), bf16),
                pltpu.VMEM((SWITCH, chunks, half, width), f32),
                pltpu.VMEM((SWITCH, chunks, full, width), f32),
                pltpu.VMEM((LEVELS - SWITCH, chunks_b, half, width_b), f32),
                pltpu.VMEM((LEVELS - SWITCH, chunks_b, full, width_b), f32),
                pltpu.VMEM((2 * full, width), bf16),
                pltpu.VMEM((chunks_b, 2, half, width_b), f32),
                pltpu.SemaphoreType.DMA((3,)),
                pltpu.SemaphoreType.DMA((chunks,)),
                pltpu.SemaphoreType.DMA((SWITCH, chunks)),
                pltpu.SemaphoreType.DMA((SWITCH, chunks)),
                pltpu.SemaphoreType.DMA((LEVELS - SWITCH, chunks_b)),
                pltpu.SemaphoreType.DMA((LEVELS - SWITCH, chunks_b)),
                pltpu.SemaphoreType.DMA((chunks_b,)),
                pltpu.SemaphoreType.REGULAR,
            ],
            compiler_params=pltpu.CompilerParams(
                collective_id=0, has_side_effects=True, vmem_limit_bytes=VMEM_BYTES
            ),
        )(factor_order, box_perm, wavefield, leaf_map, factors, closing)
        return pl.pallas_call(
            project,
            out_shape=jax.ShapeDtypeStruct(wavefield.shape, f32),
            in_specs=[in_hbm, in_hbm],
            out_specs=in_hbm,
            scratch_shapes=[
                pltpu.VMEM((chunks, 2, half, width), f32),
                pltpu.VMEM((chunks, half, width), f32),
                pltpu.SemaphoreType.DMA((chunks,)),
                pltpu.SemaphoreType.DMA((chunks,)),
                pltpu.SemaphoreType.DMA((chunks,)),
            ],
            compiler_params=pltpu.CompilerParams(vmem_limit_bytes=VMEM_BYTES),
        )(image, measured)

    return jax.shard_map(
        per_device,
        mesh=mesh,
        in_specs=(
            P(("grp", "dev"), None, None, None),
            P(("grp", "dev"), None, None),
            P(("grp", "dev"), None, None, None),
            P(None, ("grp", "dev"), None, None, None),
            P(("grp", "dev"), None, None, None),
            P(("grp", "dev"), None),
            P(),
        ),
        out_specs=P(("grp", "dev"), None, None, None),
        check_vma=False,
    )
```

time: 174 us -> 152 us (0.87)
  Pallas kernels: 171 us -> 151 us
  local copies, waits for them, and re-layouts: 3.14 us -> 0 us
    pallas_call x1, Pallas kernels: 171 us -> 148 us  [per_device(): pl.pallas_call(functools.partial(kernel, dev_bits), out_shape=jax.ShapeDt...]
    unnamed x1 -> x0, local copies, waits for them, and re-layouts: 3.14 us -> none
    pallas_call x0 -> x1, Pallas kernels: none -> 2.81 us  [per_device(): pl.pallas_call(project, out_shape=jax.ShapeDtypeStruct(wavefield.shape, f...]
where the time goes in v1:
time: 152 us; the launch traced here: 151 us
  Pallas kernels  151 us (99%)
    pallas_call x1, Pallas kernels, per_device(): pl.pallas_call(functools.partial(kernel, dev_bits), out_shape=jax.ShapeDt...  148 us

profile of v1, /device:TPU:1, one launch (start us, length us, event | category | flops | bytes accessed | tf_op | source)
XLA Modules:
  0.0 151.2 jit_solution(14370420771950142958)
XLA Ops:
  0.0 148.4 %shard_map.73.image_hbm = f32[1,2,128,2048]{3,2,1,0:T(8,128)} custom-call(s32[8]{0:T(128)} %order_ref.1, s32[1,2048]{1,0:T(1,128)} %perm_ref.1, f32[1,2,128,2048]{3,2,1,0:T(8,128)} %field_hbm.1, f32[1,2,128,128]{3,2,1,0:T(8,128)} %leaf_hbm.1, f32[8,1,2,128,128]{4,3,2,1,0:T(8,128)} %factors_hbm.1, f32[1,2,128,128]{3,2,1,0:T(8,128)} %closing_hbm.1), custom_call_target="tpu_custom_call" | custom-call | tf_op jit(solution)/shard_map/pallas_call | solution.py:364
  148.4 2.8 %shard_map.74 = f32[1,2,128,2048]{3,2,1,0:T(8,128)} custom-call(f32[1,2,128,2048]{3,2,1,0:T(8,128)} %shard_map.73.image_hbm, f32[1,128,2048]{2,1,0:T(8,128)} %measured_hbm.1), custom_call_target="tpu_custom_call" | custom-call | tf_op jit(solution)/shard_map/pallas_call | solution.py:399

commit v2 on v1

--- a/solution.py
+++ b/solution.py
@@ -13,15 +13,18 @@
 SWITCH = LEVELS // 2
 WIDTH = 256
 WIDTH_B = 128
-EARLY = 4
+EARLY = 5
 AHEAD = 3
 SPARE = 1
 BEFORE = 0
 LAG_2 = 3
-LAG_3 = 2
+LAG_3 = 3
+ROWS = 16
+FIRST = 2
+UNROLL = 2
 LAG_4 = 3
 LAG_5 = 3
-LAG_6 = 3
+LAG_6 = 2
 LAG_7 = 3
 
 
@@ -32,6 +35,7 @@
 ):
     chunks, half, width = near_out.shape[1:]
     chunks_b, _, width_b = far_out.shape[1:]
+    pieces = width // width_b
     slots = half // 2
     full = 2 * half
     f32, bf16 = jnp.float32, jnp.bfloat16
@@ -205,26 +209,42 @@
         hand_on(3, chunk, arrive(2, chunk))
         remote(3, chunk).start()
 
-    def level_3(chunk):
+    def take(chunk):
         coeffs = arrive(3, chunk)
         high = coeffs.astype(bf16)
         parts[:full] = high
         parts[full:] = (coeffs - high.astype(f32)).astype(bf16)
 
-        def place(target, carry):
-            both = jnp.dot(parts[...], onehot[target, columns(chunk), :], preferred_element_type=f32)
-            both = both[:full] + both[full:]
-            for piece in range(width // width_b):
-                which = target * (width // width_b) + piece
-                block = both[:, piece * width_b : (piece + 1) * width_b]
-                far_out[0, which] += block[:half]
-                far_held[0, which, :half] += block[half:]
+    def place(chunk, target):
+        both = jnp.dot(parts[...], onehot[target, columns(chunk), :], preferred_element_type=f32)
+        both = both[:full] + both[full:]
+        for piece in range(pieces):
+            which = target * pieces + piece
+            block = both[:, piece * width_b : (piece + 1) * width_b]
+            far_out[0, which] += block[:half]
+            far_held[0, which, :half] += block[half:]
+
+    def place_from(chunk, first):
+        def one(target, carry):
+            place(chunk, target)
             return carry
 
-        lax.fori_loop(0, chunks, place, 0, unroll=2)
+        lax.fori_loop(first, chunks, one, 0, unroll=UNROLL)
+
+    def level_3(chunk):
+        take(chunk)
+        place_from(chunk, 0)
+
+    def last_level_3():
+        take(chunks - 1)
+        for target in range(FIRST):
+            place(chunks - 1, target)
+            for piece in range(pieces):
+                remote(SWITCH, target * pieces + piece).start()
+        place_from(chunks - 1, FIRST)
 
     def switch(chunk):
-        remote(SWITCH, chunk).start()
+        pl.when(chunk >= FIRST * pieces)(lambda: remote(SWITCH, chunk).start())
 
     def middle(level, chunk):
         hand_on(level + 1, chunk, arrive(level, chunk))
@@ -254,7 +274,7 @@
         def _():
             pl.semaphore_signal(turn_sem, inc=1, device_id=partner(1), device_id_type=MESH)
 
-        when_in_range(step - LAG_3, level_3)
+        when_in_range(step - LAG_3, level_3, chunks - 1)
         return carry
 
     @pl.when(first_core)
@@ -264,7 +284,7 @@
             when_in_range(step - 1, functools.partial(send, 2))
             return along(step - LAG_2, carry)
 
-        lax.fori_loop(0, chunks + LAG_2 + LAG_3, both, 0)
+        lax.fori_loop(0, chunks - 1 + LAG_2 + LAG_3, both, 0)
 
     @pl.when(jnp.logical_not(first_core))
     def _():
@@ -284,7 +304,9 @@
             pl.when(step + AHEAD < chunks)(lambda: send(2, step + AHEAD))
             return carry
 
-        lax.fori_loop(0, chunks + LAG_3, rest, 0)
+        lax.fori_loop(0, chunks - 1 + LAG_3, rest, 0)
+
+    last_level_3()
 
     def leave(levels, chunk):
         for level in levels:
@@ -312,21 +334,19 @@
 
 
 def project(image_hbm, measured_hbm, out_hbm, image, measured, in_sem, measured_sem, out_sem):
-    chunks, _, _, width = image.shape
-
-    def columns(chunk):
-        return pl.ds(pl.multiple_of(chunk * width, width), width)
+    chunks, _, rows, _ = image.shape
+
+    def part(chunk):
+        return pl.ds(pl.multiple_of(chunk * rows, rows), rows)
 
     def get(chunk):
-        return pltpu.make_async_copy(image_hbm.at[0, :, :, columns(chunk)], image.at[chunk], in_sem.at[chunk])
+        return pltpu.make_async_copy(image_hbm.at[0, :, part(chunk)], image.at[chunk], in_sem.at[chunk])
+
+    def get_measured(chunk):
+        return pltpu.make_async_copy(measured_hbm.at[0, part(chunk)], measured.at[chunk], measured_sem.at[chunk])
 
     def put(chunk):
-        return pltpu.make_async_copy(image.at[chunk], out_hbm.at[0, :, :, columns(chunk)], out_sem.at[chunk])
-
-    def get_measured(chunk):
-        return pltpu.make_async_copy(
-            measured_hbm.at[0, :, columns(chunk)], measured.at[chunk], measured_sem.at[chunk]
-        )
+        return pltpu.make_async_copy(image.at[chunk], out_hbm.at[0, :, part(chunk)], out_sem.at[chunk])
 
     for chunk in range(chunks):
         get(chunk).start()
@@ -402,11 +422,11 @@
             in_specs=[in_hbm, in_hbm],
             out_specs=in_hbm,
             scratch_shapes=[
-                pltpu.VMEM((chunks, 2, half, width), f32),
-                pltpu.VMEM((chunks, half, width), f32),
-                pltpu.SemaphoreType.DMA((chunks,)),
-                pltpu.SemaphoreType.DMA((chunks,)),
-                pltpu.SemaphoreType.DMA((chunks,)),
+                pltpu.VMEM((half // ROWS, 2, ROWS, boxes), f32),
+                pltpu.VMEM((half // ROWS, ROWS, boxes), f32),
+                pltpu.SemaphoreType.DMA((half // ROWS,)),
+                pltpu.SemaphoreType.DMA((half // ROWS,)),
+                pltpu.SemaphoreType.DMA((half // ROWS,)),
             ],
             compiler_params=pltpu.CompilerParams(vmem_limit_bytes=VMEM_BYTES),
         )(image, measured)

time: 152 us -> 150 us (0.987)
  no operation moved by 1% of the time
where the time goes in v2:
time: 150 us
  Pallas kernels  150 us (100%)
    pallas_call x1, Pallas kernels, per_device(): pl.pallas_call(functools.partial(kernel, dev_bits), out_shape=jax.ShapeDt...  147 us

profile of v2, /device:TPU:1, one launch (start us, length us, event | category | flops | bytes accessed | tf_op | source)
XLA Modules:
  0.0 150.2 jit_solution(14937789633973869667)
XLA Ops:
  0.0 147.4 %shard_map.73.image_hbm = f32[1,2,128,2048]{3,2,1,0:T(8,128)} custom-call(s32[8]{0:T(128)} %order_ref.1, s32[1,2048]{1,0:T(1,128)} %perm_ref.1, f32[1,2,128,2048]{3,2,1,0:T(8,128)} %field_hbm.1, f32[1,2,128,128]{3,2,1,0:T(8,128)} %leaf_hbm.1, f32[8,1,2,128,128]{4,3,2,1,0:T(8,128)} %factors_hbm.1, f32[1,2,128,128]{3,2,1,0:T(8,128)} %closing_hbm.1), custom_call_target="tpu_custom_call" | custom-call | tf_op jit(solution)/shard_map/pallas_call | solution.py:384
  147.4 2.8 %shard_map.74 = f32[1,2,128,2048]{3,2,1,0:T(8,128)} custom-call(f32[1,2,128,2048]{3,2,1,0:T(8,128)} %shard_map.73.image_hbm, f32[1,128,2048]{2,1,0:T(8,128)} %measured_hbm.1), custom_call_target="tpu_custom_call" | custom-call | tf_op jit(solution)/shard_map/pallas_call | solution.py:419

commit v3 on v2

--- a/solution.py
+++ b/solution.py
@@ -29,8 +29,8 @@
 
 
 def kernel(
-    dev_bits, order_ref, perm_ref, field_hbm, leaf_hbm, factors_hbm, closing_hbm, image_hbm,
-    field, leaf, factors, closing, weights, onehot, near_out, near_held, far_out, far_held, parts, image,
+    dev_bits, order_ref, perm_ref, field_hbm, measured_hbm, leaf_hbm, factors_hbm, closing_hbm, image_hbm,
+    field, measured, leaf, factors, closing, weights, onehot, near_out, near_held, far_out, far_held, parts, image,
     in_sem, chunk_sem, near_send, near_recv, far_send, far_recv, out_sem, turn_sem,
 ):
     chunks, half, width = near_out.shape[1:]
@@ -96,6 +96,8 @@
     fetch_factors.start()
     fetch_closing = pltpu.make_async_copy(closing_hbm.at[0], closing, in_sem.at[2])
     fetch_closing.start()
+    fetch_measured = pltpu.make_async_copy(measured_hbm.at[0], measured, in_sem.at[3])
+    fetch_measured.start()
 
     def store_weights(which, row, left, right):
         rows = left.shape[0]
@@ -137,6 +139,10 @@
     def product(which, vectors):
         high = vectors.astype(bf16)
         low = (vectors - high.astype(f32)).astype(bf16)
+        count = vectors.shape[1]
+        if count <= 128:
+            all_four = jnp.dot(weights[which], jnp.concatenate([high, low], axis=1), preferred_element_type=f32)
+            return all_four[:full, :count] + (all_four[full:, :count] + all_four[:full, count:])
         both = jnp.dot(weights[which], high, preferred_element_type=f32)
         rest = jnp.dot(weights[which, :full], low, preferred_element_type=f32)
         return both[:full] + (both[full:] + rest)
@@ -184,6 +190,7 @@
         return carry
 
     lax.fori_loop(0, chunks * chunks, fill_onehot, 0)
+    fetch_measured.wait()
 
     def clear(chunk, carry):
         hand_on(SWITCH, chunk, jnp.zeros((full, width_b), f32))
@@ -252,8 +259,10 @@
 
     def level_7(chunk):
         coeffs = arrive(7, chunk)
-        image[chunk, 0] = coeffs[:half]
-        image[chunk, 1] = coeffs[half:]
+        real, imag = coeffs[:half], coeffs[half:]
+        scale = measured[:, columns(chunk, width_b)] * lax.rsqrt(jnp.maximum(real * real + imag * imag, 0.25))
+        image[chunk, 0] = real * scale
+        image[chunk, 1] = imag * scale
         put_image(chunk).start()
 
     first_core = grp % 2 == 0
@@ -333,41 +342,18 @@
     lax.fori_loop(0, chunks_b, finish, 0)
 
 
-def project(image_hbm, measured_hbm, out_hbm, image, measured, in_sem, measured_sem, out_sem):
-    chunks, _, rows, _ = image.shape
-
-    def part(chunk):
-        return pl.ds(pl.multiple_of(chunk * rows, rows), rows)
-
-    def get(chunk):
-        return pltpu.make_async_copy(image_hbm.at[0, :, part(chunk)], image.at[chunk], in_sem.at[chunk])
-
-    def get_measured(chunk):
-        return pltpu.make_async_copy(measured_hbm.at[0, part(chunk)], measured.at[chunk], measured_sem.at[chunk])
-
-    def put(chunk):
-        return pltpu.make_async_copy(image.at[chunk], out_hbm.at[0, :, part(chunk)], out_sem.at[chunk])
-
-    for chunk in range(chunks):
-        get(chunk).start()
-        get_measured(chunk).start()
-
-    def step(chunk, carry):
-        get(chunk).wait()
-        get_measured(chunk).wait()
-        real, imag = image[chunk, 0], image[chunk, 1]
-        scale = measured[chunk] * lax.rsqrt(jnp.maximum(real * real + imag * imag, 0.25))
-        image[chunk, 0] = real * scale
-        image[chunk, 1] = imag * scale
-        put(chunk).start()
-        return carry
-
-    def finish(chunk, carry):
-        put(chunk).wait()
-        return carry
-
-    lax.fori_loop(0, chunks, step, 0)
-    lax.fori_loop(0, chunks, finish, 0)
+def pass_on(source, target, buffer, in_sem, out_sem):
+    parts, _, rows, _ = buffer.shape
+    for part in range(parts):
+        where = pl.ds(part * rows, rows)
+        pltpu.make_async_copy(source.at[0, :, where], buffer.at[part], in_sem.at[part]).start()
+    for part in range(parts):
+        where = pl.ds(part * rows, rows)
+        pltpu.make_async_copy(source.at[0, :, where], buffer.at[part], in_sem.at[part]).wait()
+        pltpu.make_async_copy(buffer.at[part], target.at[0, :, where], out_sem.at[part]).start()
+    for part in range(parts):
+        where = pl.ds(part * rows, rows)
+        pltpu.make_async_copy(buffer.at[part], target.at[0, :, where], out_sem.at[part]).wait()
 
 
 def solution(mesh):
@@ -388,10 +374,11 @@
                 pl.BlockSpec(memory_space=pltpu.SMEM),
                 in_vmem,
             ]
-            + [in_hbm] * 4,
+            + [in_hbm] * 5,
             out_specs=in_hbm,
             scratch_shapes=[
                 pltpu.VMEM((2, half, boxes), f32),
+                pltpu.VMEM((half, boxes), f32),
                 pltpu.VMEM((2, half, half), f32),
                 pltpu.VMEM((LEVELS, 2, half, half), f32),
                 pltpu.VMEM((2, half, half), f32),
@@ -403,7 +390,7 @@
                 pltpu.VMEM((LEVELS - SWITCH, chunks_b, full, width_b), f32),
                 pltpu.VMEM((2 * full, width), bf16),
                 pltpu.VMEM((chunks_b, 2, half, width_b), f32),
-                pltpu.SemaphoreType.DMA((3,)),
+                pltpu.SemaphoreType.DMA((4,)),
                 pltpu.SemaphoreType.DMA((chunks,)),
                 pltpu.SemaphoreType.DMA((SWITCH, chunks)),
                 pltpu.SemaphoreType.DMA((SWITCH, chunks)),
@@ -415,21 +402,19 @@
             compiler_params=pltpu.CompilerParams(
                 collective_id=0, has_side_effects=True, vmem_limit_bytes=VMEM_BYTES
             ),
-        )(factor_order, box_perm, wavefield, leaf_map, factors, closing)
+        )(factor_order, box_perm, wavefield, measured, leaf_map, factors, closing)
         return pl.pallas_call(
-            project,
+            pass_on,
             out_shape=jax.ShapeDtypeStruct(wavefield.shape, f32),
-            in_specs=[in_hbm, in_hbm],
+            in_specs=[in_hbm],
             out_specs=in_hbm,
             scratch_shapes=[
                 pltpu.VMEM((half // ROWS, 2, ROWS, boxes), f32),
-                pltpu.VMEM((half // ROWS, ROWS, boxes), f32),
-                pltpu.SemaphoreType.DMA((half // ROWS,)),
                 pltpu.SemaphoreType.DMA((half // ROWS,)),
                 pltpu.SemaphoreType.DMA((half // ROWS,)),
             ],
             compiler_params=pltpu.CompilerParams(vmem_limit_bytes=VMEM_BYTES),
-        )(image, measured)
+        )(image)
 
     return jax.shard_map(
         per_device,

time: 150 us -> 150 us (level)
  no operation moved by 1% of the time
where the time goes in v3:
time: 150 us; the launch traced here: 149 us
  Pallas kernels  149 us (99%)
    pallas_call x1, Pallas kernels, per_device(): pl.pallas_call(functools.partial(kernel, dev_bits), out_shape=jax.ShapeDt...  147 us

profile of v3, /device:TPU:1, one launch (start us, length us, event | category | flops | bytes accessed | tf_op | source)
XLA Modules:
  0.0 149.5 jit_solution(11676853801007567943)
XLA Ops:
  0.0 147.1 %shard_map.73.source = f32[1,2,128,2048]{3,2,1,0:T(8,128)} custom-call(s32[8]{0:T(128)} %order_ref.1, s32[1,2048]{1,0:T(1,128)} %perm_ref.1, f32[1,2,128,2048]{3,2,1,0:T(8,128)} %field_hbm.1, f32[1,128,2048]{2,1,0:T(8,128)} %measured_hbm.1, f32[1,2,128,128]{3,2,1,0:T(8,128)} %leaf_hbm.1, f32[8,1,2,128,128]{4,3,2,1,0:T(8,128)} %factors_hbm.1, ...), custom_call_target="tpu_custom_call" | custom-call | tf_op jit(solution)/shard_map/pallas_call | solution.py:370
  147.1 2.4 %shard_map.74 = f32[1,2,128,2048]{3,2,1,0:T(8,128)} custom-call(f32[1,2,128,2048]{3,2,1,0:T(8,128)} %shard_map.73.source), custom_call_target="tpu_custom_call" | custom-call | tf_op jit(solution)/shard_map/pallas_call | solution.py:406

commit v4 on v3

--- a/solution.py
+++ b/solution.py
@@ -22,9 +22,9 @@
 ROWS = 16
 FIRST = 2
 UNROLL = 2
-LAG_4 = 3
+LAG_4 = 2
 LAG_5 = 3
-LAG_6 = 2
+LAG_6 = 3
 LAG_7 = 3
 
 

time: 150 us -> 150 us (level)
  no operation moved by 1% of the time
where the time goes in v4:
time: 150 us
  Pallas kernels  150 us (100%)
    pallas_call x1, Pallas kernels, per_device(): pl.pallas_call(functools.partial(kernel, dev_bits), out_shape=jax.ShapeDt...  147 us

profile of v4, /device:TPU:1, one launch (start us, length us, event | category | flops | bytes accessed | tf_op | source)
XLA Modules:
  0.0 149.6 jit_solution(3639165202730642126)
XLA Ops:
  0.0 147.2 %shard_map.73.source = f32[1,2,128,2048]{3,2,1,0:T(8,128)} custom-call(s32[8]{0:T(128)} %order_ref.1, s32[1,2048]{1,0:T(1,128)} %perm_ref.1, f32[1,2,128,2048]{3,2,1,0:T(8,128)} %field_hbm.1, f32[1,128,2048]{2,1,0:T(8,128)} %measured_hbm.1, f32[1,2,128,128]{3,2,1,0:T(8,128)} %leaf_hbm.1, f32[8,1,2,128,128]{4,3,2,1,0:T(8,128)} %factors_hbm.1, ...), custom_call_target="tpu_custom_call" | custom-call | tf_op jit(solution)/shard_map/pallas_call | solution.py:370
  147.2 2.4 %shard_map.74 = f32[1,2,128,2048]{3,2,1,0:T(8,128)} custom-call(f32[1,2,128,2048]{3,2,1,0:T(8,128)} %shard_map.73.source), custom_call_target="tpu_custom_call" | custom-call | tf_op jit(solution)/shard_map/pallas_call | solution.py:406
